TPU v7x, 256 devices: a whole 4x4x8 slice. The times are simulated.
256 devices in a mesh: dp: 32 (over z, y), seq: 8 (over x, core).
Axes of the slice: x: 4, y: 4, z: 8, core: 2. Of those that a mesh axis runs over, the one named last changes fastest.
Arguments:
- prefill_queries: bfloat16 [32768, 4096], P(('dp', 'seq')), may hold values from -8 to 8
- prefill_key_values: bfloat16 [32768, 2048], P(('dp', 'seq')), may hold values from -8 to 8
- decode_queries: bfloat16 [32, 4096], P('dp', 'seq'), may hold values from -8 to 8
- decode_key_values: bfloat16 [32, 2048], P('dp', 'seq'), may hold values from -8 to 8
- arrival: int32 [32], replicated, may hold values from 0 to 31, as said below
- pooled_key_values: bfloat16 [1024, 128, 2048], P('dp', None, 'seq'), may hold values from -8 to 8
- page_table: int32 [32, 32], P('dp'), may hold values from 0 to 31, as said below
- cache_len: int32 [32], P('dp'), may hold values from 1 to 4096, as said below
- mover: int32 [32], P('dp'), may hold values from 0 to 0, as said below
Outputs:
- prefill_out: bfloat16 [32768, 4096], P(('dp', 'seq'))
- decode_out: bfloat16 [32, 4096], P('dp', 'seq')
- received_pages: bfloat16 [1024, 128, 2048], P('dp', None, 'seq')
Inputs may be any that keep to these rules, and one draw needn't show every extreme that they name: `arrival`: every decode request appears exactly once. `page_table`: the 1 request of one group together name each of that group's 32 pages exactly once. `cache_len`: some request has exactly 4096 cached tokens in every draw. `mover`: the request with the most cached tokens always moves.
All inputs are finite; a program needn't handle non-finite values.
Results may differ from a plain program's by a relative error of at most 0.006.
Values may be sent and summed in bfloat16 or wider, within the bound.
A program may use at most 64 MiB of HBM per device.

v0:
```python
import math
import jax
import jax.numpy as jnp
from jax import lax
from jax.sharding import PartitionSpec as P

QUERY_HEADS = 32
KV_HEAD_COUNT = 8
HEAD_SIZE = 128
NEG_FILL = -1e30


def passed_along(block, axis, distance):
    devices = range(lax.axis_size(axis))
    route = [((i - distance) % len(devices), i) for i in devices]
    return lax.ppermute(block, axis, route)


def keys_attention(prefill_queries, prefill_key_values):
    group_local_rows = prefill_queries.shape[0]
    group_extent = QUERY_HEADS // KV_HEAD_COUNT
    query_rows = prefill_queries.reshape(group_local_rows, KV_HEAD_COUNT, group_extent, HEAD_SIZE)
    row_offset = lax.axis_index("seq") * group_local_rows
    scale_factor = 1.0 / math.sqrt(HEAD_SIZE)
    query_pos = row_offset + lax.broadcasted_iota(jnp.int32, (group_local_rows, 1), 0)
    state_dimensions = (KV_HEAD_COUNT, group_extent, group_local_rows)
    portion_slice = lax.all_gather(prefill_key_values, "seq", axis=0, tiled=True)
    first_index = jnp.int32(0)
    run_max = jnp.full(state_dimensions, NEG_FILL, jnp.float32)
    run_total = jnp.zeros(state_dimensions, jnp.float32)
    run_acc = jnp.zeros(state_dimensions + (HEAD_SIZE,), jnp.float32)
    portion_rows = portion_slice.shape[0]
    key_value_rows = portion_slice.reshape(portion_rows, KV_HEAD_COUNT, 2 * HEAD_SIZE)
    for first_key in range(0, portion_rows, 512):
        width_now = min(512, portion_rows - first_key)
        key_block = key_value_rows[first_key : first_key + width_now]
        scores = (
            jnp.einsum(
                "qngd,knd->ngqk",
                query_rows,
                key_block[:, :, :HEAD_SIZE],
                preferred_element_type=jnp.float32,
            )
            * scale_factor
        )
        key_pos = first_index + first_key + lax.broadcasted_iota(jnp.int32, (1, width_now), 1)
        allowed = key_pos <= query_pos
        masked = jnp.where(allowed, scores, NEG_FILL)
        new_max = jnp.maximum(run_max, jnp.max(masked, axis=-1))
        rescale = jnp.exp(run_max - new_max)
        weights = jnp.where(allowed, jnp.exp(masked - new_max[..., None]), 0.0).astype(jnp.bfloat16)
        run_total = run_total * rescale + jnp.sum(weights, axis=-1, dtype=jnp.float32)
        run_acc = run_acc * rescale[..., None] + jnp.einsum(
            "ngqk,knd->ngqd",
            weights,
            key_block[:, :, HEAD_SIZE:],
            preferred_element_type=jnp.float32,
        )
        run_max = new_max
    normed = run_acc / run_total[..., None]
    return (
        jnp.transpose(normed, (2, 0, 1, 3))
        .astype(jnp.bfloat16)
        .reshape(group_local_rows, QUERY_HEADS * HEAD_SIZE)
    )


def decode_attention(
    decode_queries, decode_key_values, arrival, pooled_key_values, page_table, cache_len
):
    request_count = decode_queries.shape[0]
    kv_local = decode_key_values.shape[1] // (2 * HEAD_SIZE)
    group_extent = QUERY_HEADS // KV_HEAD_COUNT
    query_all, pair_all = (
        lax.all_gather(decode_queries, "dp", axis=0, tiled=True),
        lax.all_gather(decode_key_values, "dp", axis=0, tiled=True),
    )
    total_rows = query_all.shape[0]
    wanted = lax.axis_index("dp") * request_count + lax.broadcasted_iota(
        jnp.int32, (request_count, 1), 0
    )
    row_ids = lax.broadcasted_iota(jnp.int32, (request_count, total_rows), 1)
    decode_row = jnp.sum(jnp.where(arrival[None, :] == wanted, row_ids, 0), axis=1)
    query_sel = jnp.take(query_all, decode_row, axis=0).reshape(
        request_count, kv_local, group_extent, HEAD_SIZE
    )
    pair_sel = jnp.take(pair_all, decode_row, axis=0).reshape(
        request_count, kv_local, 2 * HEAD_SIZE
    )
    cache_row_list = jnp.take(pooled_key_values, page_table, axis=0)
    cache_row_list = cache_row_list.reshape(request_count, -1, kv_local, 2 * HEAD_SIZE)
    span_rows = cache_row_list.shape[1]
    scale_factor = 1.0 / math.sqrt(HEAD_SIZE)
    cached_scores = (
        jnp.einsum(
            "rngd,rtnd->rngt",
            query_sel,
            cache_row_list[..., :HEAD_SIZE],
            preferred_element_type=jnp.float32,
        )
        * scale_factor
    )
    new_scores = (
        jnp.einsum(
            "rngd,rnd->rng",
            query_sel,
            pair_sel[..., :HEAD_SIZE],
            preferred_element_type=jnp.float32,
        )
        * scale_factor
    )
    valid_rows = (
        lax.broadcasted_iota(jnp.int32, (request_count, 1, 1, span_rows), 3)
        < cache_len[:, None, None, None]
    )
    masked = jnp.where(valid_rows, cached_scores, NEG_FILL)
    row_max = jnp.maximum(jnp.max(masked, axis=-1), new_scores)
    cached_weights = jnp.where(valid_rows, jnp.exp(masked - row_max[..., None]), 0.0).astype(
        jnp.bfloat16
    )
    new_weights = jnp.exp(new_scores - row_max).astype(jnp.bfloat16)
    wide_new = new_weights.astype(jnp.float32)
    totals = jnp.sum(cached_weights, axis=-1, dtype=jnp.float32) + wide_new
    summed = jnp.einsum(
        "rngt,rtnd->rngd",
        cached_weights,
        cache_row_list[..., HEAD_SIZE:],
        preferred_element_type=jnp.float32,
    )
    summed = (
        summed + wide_new[..., None] * pair_sel[..., HEAD_SIZE:].astype(jnp.float32)[:, :, None, :]
    )
    return (
        (summed / totals[..., None])
        .astype(jnp.bfloat16)
        .reshape(request_count, kv_local * group_extent * HEAD_SIZE)
    )


def move_pages(pooled_key_values, page_table, cache_len, mover):
    mover_slot = mover[0]
    moving_table = lax.dynamic_index_in_dim(page_table, mover_slot, 0, keepdims=False)
    moving_len = lax.dynamic_index_in_dim(cache_len, mover_slot, 0, keepdims=False)
    page_rows = jnp.take(pooled_key_values, moving_table, axis=0)
    live_pages = (
        lax.broadcasted_iota(jnp.int32, (page_rows.shape[0], 1, 1), 0) * page_rows.shape[1]
        < moving_len
    )
    page_rows = jnp.where(live_pages, page_rows, jnp.zeros_like(page_rows))
    return passed_along(page_rows, "dp", 1)


def on_device(
    prefill_queries,
    prefill_key_values,
    decode_queries,
    decode_key_values,
    arrival,
    pooled_key_values,
    page_table,
    cache_len,
    mover,
):
    prefill_out = keys_attention(prefill_queries, prefill_key_values)
    decode_out = decode_attention(
        decode_queries, decode_key_values, arrival, pooled_key_values, page_table, cache_len
    )
    received_pages = move_pages(pooled_key_values, page_table, cache_len, mover)
    return (prefill_out, decode_out, received_pages)


def solution(mesh):
    placed = (
        P(("dp", "seq"), None),
        P(("dp", "seq"), None),
        P("dp", "seq"),
        P("dp", "seq"),
        P(),
        P("dp", None, "seq"),
        P("dp", None),
        P("dp"),
        P("dp"),
    )
    return jax.shard_map(
        on_device,
        mesh=mesh,
        in_specs=placed,
        out_specs=(P(("dp", "seq"), None), P("dp", "seq"), P("dp", None, "seq")),
        check_vma=False,
    )
```

profile of v0, /device:TPU:6, one launch (start us, length us, event | category | flops | bytes accessed | tf_op | source)
XLA Modules:
  0.0 181.2 jit_solution(11569675293962441517)
XLA Ops:
  7.2 0.0 copy-start
  7.2 0.0 copy-start.3
  7.2 0.0 all-gather.4.cloned.1.call-start
  7.2 2.2 %copy.26 = bf16[128,2048]{0,1:T(8,128)(2,1)} copy(bf16[128,2048]{1,0:T(8,128)(2,1)} %param.10) | data formatting | bytes 1048576 | tf_op args[1]
  9.4 0.0 all-gather.4.cloned.1.call-update
  10.1 0.7 fusion.23
  10.8 0.0 copy-done
  10.8 2.0 %gather_fusion.1 = bf16[32,128,256]{2,1,0:T(8,128)(2,1)} fusion(bf16[32,128,256]{2,1,0:T(8,128)(2,1)S(1)} %copy-done, s32[1024]{0:T(1024)S(1)} %pad_clamp_fusion), kind=kCustom, calls=%fused_computation.1 | custom fusion | bytes 4194432 | tf_op jit(solution)/shard_map/jit(_take)/gather | solution.py:144
  12.8 0.0 copy-done.3
  12.8 3.3 %select_select_fusion = bf16[32,128,256]{2,1,0:T(8,128)(2,1)} fusion(bf16[32,128,256]{2,1,0:T(8,128)(2,1)} %gather_fusion.1, pred[32]{0:T(512)(128)(4,1)S(1)} %get-tuple-element.57, pred[32]{0:T(512)(128)(4,1)S(1)} %get-tuple-element.58), kind=kLoop, calls=%fused_computation.17 | loop fusion | flops 2097152 | bytes 4194368 | tf_op jit(solution)/shard_map/jit(_where)/select_n | solution.py:149
  16.0 1.6 collective-permute-start
  17.6 1.8 reshape.261
  19.4 0.0 copy-start.4
  19.5 0.0 copy-start.1
  19.5 0.0 copy-start.2
  19.5 2.0 %gather_fusion = bf16[32,128,256]{2,1,0:T(8,128)(2,1)} fusion(bf16[32,128,256]{2,1,0:T(8,128)(2,1)S(1)} %copy-done, s32[1024]{0:T(1024)S(1)} %pad_clamp_fusion.1), kind=kCustom, calls=%fused_computation | custom fusion | bytes 4194432 | tf_op jit(solution)/shard_map/jit(_take)/gather | solution.py:90
  21.5 0.1 broadcast_bitcast_fusion
  21.6 1.9 %broadcast_select_fusion = bf16[1,4096,1,256]{3,1,2,0:T(8,128)(2,1)S(1)} fusion(bf16[1,4096,1,256]{3,1,2,0:T(8,128)(2,1)} %bitcast.141, pred[4096]{0:T(1024)(128)(4,1)S(1)} %broadcast_bitcast_fusion), kind=kLoop, calls=%fused_computation.18 | loop fusion | flops 1048576 | bytes 4198400 | tf_op jit(solution)/shard_map/jit(_take)/select_n | solution.py:90
  23.5 0.0 copy-done.4
  23.5 0.6 fusion.22
  26.1 0.0 copy-done.1
  26.1 84.3 %all-gather = bf16[32,1,512]{2,1,0:T(2,128)(2,1)S(1)} all-gather(bf16[1,1,512]{2,1,0:T(2,128)(2,1)S(1)} %bitcast.147), channel_id=1, replica_groups=mesh['dp'=32,'seq'=8] {'dp'}, dimensions={0}, use_global_device_ids=true | all-gather | bytes 33792 | tf_op jit(solution)/shard_map/all_gather | solution.py:75
  110.4 0.0 copy-done.2
  110.4 41.7 %all-gather.1 = bf16[32,1,256]{2,1,0:T(2,128)(2,1)S(1)} all-gather(bf16[1,1,256]{2,1,0:T(2,128)(2,1)S(1)} %bitcast.149), channel_id=1, replica_groups=mesh['dp'=32,'seq'=8] {'dp'}, dimensions={0}, use_global_device_ids=true | all-gather | bytes 16896 | tf_op jit(solution)/shard_map/all_gather | solution.py:76
  152.2 0.5 fusion.30
  152.7 0.1 fusion.31
  152.8 0.2 convert_reduce_fusion.2
  153.0 0.3 fusion.8
  153.3 0.6 copy.52
  153.9 0.1 broadcast_compare_fusion
  154.0 0.0 collective-permute-done
  154.0 0.0 all-gather.4.cloned.1.call-done
  154.1 2.5 %fusion.29 = (bf16[512,2048]{0,1:T(8,128)(2,1)S(1)}, bf16[512,2048]{0,1:T(8,128)(2,1)S(1)}) fusion(bf16[1024,2048]{0,1:T(8,128)(2,1)} %all-gather.4.cloned.1.call-done), kind=kLoop, calls=%fused_computation.77 | loop fusion | bytes 8388608 | tf_op jit(solution)/shard_map/slice | solution.py:36
  156.6 2.1 %fusion = (f32[8,4,128]{2,1,0:T(4,128)S(1)}, f32[8,512,128,4]{2,1,3,0:T(8,128)S(1)}) fusion(pred[128,512]{0,1:T(8,128)(4,1)S(1)} %get-tuple-element.46, bf16[128,8,4,128]{3,2,1,0:T(4,128)(2,1)S(1)} %reshape.261, bf16[512,8,256]{0,2,1:T(8,128)(2,1)S(1)} %bitcast.144), kind=kOutput, calls=%fused_computation.8 | convolution fusion | flops 543158272 | bytes 10567680 | tf_op jit(solution)/shard_map/qngd,knd->ngqk/dot_general | solution.py:38
  158.6 2.1 %fusion.1 = (f32[8,4,128]{2,1,0:T(4,128)S(1)}, f32[8,512,128,4]{2,1,3,0:T(8,128)S(1)}) fusion(pred[128,512]{0,1:T(8,128)(4,1)S(1)} %get-tuple-element.45, bf16[128,8,4,128]{3,2,1,0:T(4,128)(2,1)S(1)} %reshape.261, bf16[512,8,256]{0,2,1:T(8,128)(2,1)S(1)} %bitcast.142), kind=kOutput, calls=%fused_computation.9 | convolution fusion | flops 543158272 | bytes 10567680 | tf_op jit(solution)/shard_map/qngd,knd->ngqk/dot_general | solution.py:38
  160.7 2.2 %fusion.11 = f32[8,4,128,128]{2,3,1,0:T(8,128)S(1)} fusion(bf16[512,8,256]{0,2,1:T(8,128)(2,1)S(1)} %bitcast.145, f32[8,512,128,4]{2,1,3,0:T(8,128)S(1)} %get-tuple-element.50, f32[8,4,128]{2,1,0:T(4,128)S(1)} %get-tuple-element.44, pred[128,512]{0,1:T(8,128)(4,1)S(1)} %get-tuple-element.46), kind=kOutput, calls=%fused_computation.31 | convolution fusion | flops 547356672 | bytes 11616256 | tf_op jit(solution)/shard_map/ngqk,knd->ngqd/dot_general | solution.py:53
  162.9 4.5 %convert_reduce_fusion = (f32[8,4,128]{2,1,0:T(4,128)S(1)}, f32[8,4,128]{2,1,0:T(4,128)S(1)}) fusion(f32[8,4,128]{2,1,0:T(4,128)S(1)} %get-tuple-element.43, f32[8,512,128,4]{2,1,3,0:T(8,128)S(1)} %get-tuple-element.48, pred[128,512]{0,1:T(8,128)(4,1)S(1)} %get-tuple-element.45, f32[8,4,128]{2,1,0:T(4,128)S(1)} %get-tuple-element.44, ...), kind=kLoop, calls=%fused_computation.4 | loop fusion | flops 29351936 | bytes 16973824 | tf_op jit(solution)/shard_map/reduce_sum | solution.py:52
  167.4 2.5 %fusion.4 = bf16[128,8,4,128]{0,3,2,1:T(8,128)(2,1)S(1)} fusion(f32[8,4,128,128]{2,3,1,0:T(8,128)S(1)} %fusion.11, bf16[512,8,256]{0,2,1:T(8,128)(2,1)S(1)} %bitcast.143, f32[128,8,4]{0,2,1:T(4,128)S(1)} %get-tuple-element.38, f32[128,8,4]{0,2,1:T(4,128)S(1)} %get-tuple-element.39, f32[128,8,4]{0,2,1:T(4,128)S(1)} %get-tuple-element.42, ...), kind=kOutput, calls=%fused_computation.14 | convolution fusion | flops 549978112 | bytes 12713984 | tf_op jit(solution)/shard_map/ngqk,knd->ngqd/dot_general | solution.py:53
  169.9 1.3 copy.33
  171.2 3.1 %copy.55 = bf16[32,128,256]{2,1,0:T(8,128)(2,1)} copy(bf16[32,128,256]{2,1,0:T(8,128)(2,1)} %collective-permute-done) | data formatting | bytes 4194304
  (14 shorter events, 0.1 us)
Async XLA Ops:
  7.2 3.6 %copy-start = (bf16[32,128,256]{2,1,0:T(8,128)(2,1)S(1)}, bf16[32,128,256]{2,1,0:T(8,128)(2,1)}, u32[]{:S(2)}) copy-start(bf16[32,128,256]{2,1,0:T(8,128)(2,1)} %param.14) | copy-start | bytes 6291460
  7.2 5.6 %copy-start.3 = (s32[1,32]{1,0:T(1,128)S(1)}, s32[1,32]{1,0:T(1,128)}, u32[]{:S(2)}) copy-start(s32[1,32]{1,0:T(1,128)} %param.15) | copy-start | bytes 388
  7.2 146.9 %all-gather.4.cloned.1.call-start = ((), (), s32[]{:S(2)}) async-start(), calls=%async_computation | async-start | bytes 4718592 | tf_op jit(solution)/shard_map/all_gather | solution.py:27
  16.0 138.0 %collective-permute-start = (bf16[32,128,256]{2,1,0:T(8,128)(2,1)}, bf16[32,128,256]{2,1,0:T(8,128)(2,1)}, u32[]{:S(2)}, u32[]{:S(2)}) collective-permute-start(bf16[32,128,256]{2,1,0:T(8,128)(2,1)} %select_select_fusion), channel_id=1, source_target_pairs={{248,0},{0,8},{8,16},{16,24},{24,32},{32,40},{40,48},{48,56},{56,6... | collective-permute-start | bytes 6291464 | tf_op jit(solution)/shard_map/ppermute | solution.py:16
  19.4 4.1 %copy-start.4 = (s32[32]{0:T(128)S(1)}, s32[32]{0:T(128)}, u32[]{:S(2)}) copy-start(s32[32]{0:T(128)} %param.13) | copy-start | bytes 388
  19.5 6.7 %copy-start.1 = (bf16[1,512]{1,0:T(2,128)(2,1)S(1)}, bf16[1,512]{1,0:T(2,128)(2,1)}, u32[]{:S(2)}) copy-start(bf16[1,512]{1,0:T(2,128)(2,1)} %param.11) | copy-start | bytes 3076
  19.5 90.9 %copy-start.2 = (bf16[1,256]{1,0:T(2,128)(2,1)S(1)}, bf16[1,256]{1,0:T(2,128)(2,1)}, u32[]{:S(2)}) copy-start(bf16[1,256]{1,0:T(2,128)(2,1)} %param.12) | copy-start | bytes 1540
Sparse Core Ops, SparseCore 0:
  10.4 40.1 all-gather.3
where the time goes:
time: 182 us; the launch traced here: 181 us
  blocking collectives  126 us (69%)
  between operations  16.8 us (9%)
  local copies, waits for them, and re-layouts  15.6 us (9%)
  other arithmetic  11.5 us (6%)
  matrix products  9.69 us (5%)
    all_gather x1, blocking collectives, decode_attention(): lax.all_gather(decode_queries, 'dp', axis=0, tiled=True)  84.3 us
    all_gather x1, blocking collectives, decode_attention(): lax.all_gather(decode_key_values, 'dp', axis=0, tiled=True)  41.7 us
    unnamed x14, local copies, waits for them, and re-layouts  7.25 us
    dot_general x2, matrix products, keys_attention(): jnp.einsum('ngqk,knd->ngqd', weights, key_block[:, :, HEAD_SIZE:], prefer...  4.67 us
    reduce_sum x1, other arithmetic, keys_attention(): jnp.sum(weights, axis=-1, dtype=jnp.float32)  4.47 us
    dot_general x2, matrix products, keys_attention(): jnp.einsum('qngd,knd->ngqk', query_rows, key_block[:, :, :HEAD_SIZE], pre...  4.16 us
  transfers between devices with their start and end apart: 2, of which 0 were waited for; matrix products, arithmetic and copies ran while one was open for 8% of the time, Pallas kernels for 0%

commit v1 on v0

--- a/solution.py
+++ b/solution.py
@@ -72,7 +72,9 @@
     kv_local = decode_key_values.shape[1] // (2 * HEAD_SIZE)
     group_extent = QUERY_HEADS // KV_HEAD_COUNT
     query_all, pair_all = (
-        lax.all_gather(decode_queries, "dp", axis=0, tiled=True),
+        jnp.concatenate(
+            lax.all_to_all(jnp.stack([decode_queries] * lax.axis_size("dp")), "dp", 0, 0), axis=0
+        ),
         lax.all_gather(decode_key_values, "dp", axis=0, tiled=True),
     )
     total_rows = query_all.shape[0]

time: 182 us -> 150 us (0.82)
  blocking collectives: 126 us -> 76.1 us
  starting transfers between devices: 1.61 us -> 13.3 us
  other arithmetic: 11.5 us -> 14 us
  matrix products: 9.69 us -> 12.1 us
    all_gather x1 -> x0, blocking collectives: 84.3 us -> none  [decode_attention(): lax.all_gather(decode_queries, 'dp', axis=0, tiled=True)]
    all_gather x1, blocking collectives: 41.7 us -> 76.1 us  [decode_attention(): lax.all_gather(decode_key_values, 'dp', axis=0, tiled=True)]
    all_to_all x0 -> x1, starting transfers between devices: none -> 11.5 us  [decode_attention(): lax.all_to_all(jnp.stack([decode_queries] * lax.axis_size('dp')), 'dp', 0...]
  transfers between devices with their start and end apart: 2 -> 3, of which waited for: 0 -> 0; matrix products, arithmetic and copies ran while one was open for 8% -> 14% of each run, Pallas kernels for 0% -> 0%
where the time goes in v1:
time: 150 us; the launch traced here: 149 us
  blocking collectives  76.1 us (51%)
  local copies, waits for them, and re-layouts  16.8 us (11%)
  between operations  16.8 us (11%)
  other arithmetic  14 us (9%)
  starting transfers between devices  13.3 us (9%)
  matrix products  12.1 us (8%)
    all_gather x1, blocking collectives, decode_attention(): lax.all_gather(decode_key_values, 'dp', axis=0, tiled=True)  76.1 us
    all_to_all x1, starting transfers between devices, decode_attention(): lax.all_to_all(jnp.stack([decode_queries] * lax.axis_size('dp')), 'dp', 0...  11.5 us
    unnamed x14, local copies, waits for them, and re-layouts  7.88 us
    dot_general x2, matrix products, keys_attention(): jnp.einsum('ngqk,knd->ngqd', weights, key_block[:, :, HEAD_SIZE:], prefer...  4.67 us
    reduce_sum x1, other arithmetic, keys_attention(): jnp.sum(weights, axis=-1, dtype=jnp.float32)  4.47 us
    dot_general x2, matrix products, keys_attention(): jnp.einsum('qngd,knd->ngqk', query_rows, key_block[:, :, :HEAD_SIZE], pre...  4.15 us
    select_n x1, other arithmetic, move_pages(): page_rows = jnp.where(live_pages, page_rows, jnp.zeros_like(page_rows))  3.32 us
  transfers between devices with their start and end apart: 3, of which 0 were waited for; matrix products, arithmetic and copies ran while one was open for 14% of the time, Pallas kernels for 0%

profile of v1, /device:TPU:6, one launch (start us, length us, event | category | flops | bytes accessed | tf_op | source)
XLA Modules:
  0.0 149.1 jit_solution(9238252749632036468)
XLA Ops:
  7.2 0.0 copy-start
  7.2 0.0 copy-start.2
  7.2 0.0 all-gather.3.cloned.1.call-start
  7.2 2.2 %copy.26 = bf16[128,2048]{0,1:T(8,128)(2,1)} copy(bf16[128,2048]{1,0:T(8,128)(2,1)} %param.10) | data formatting | bytes 1048576 | tf_op args[1]
  9.4 0.0 all-gather.3.cloned.1.call-update
  9.4 0.7 reduce.6
  10.2 0.5 broadcast.286
  10.7 0.8 reduce.9
  11.5 0.6 reshape.358
  12.1 11.5 %all-to-all-start = ((bf16[32,2,256]{2,1,0:T(2,128)(2,1)}), bf16[32,2,256]{2,1,0:T(2,128)(2,1)S(1)}, u32[]{:S(2)}, u32[]{:S(2)}) async-start(bf16[32,2,256]{2,1,0:T(2,128)(2,1)} %reshape.358), calls=%async_computation | async-start | bytes 65536 | tf_op jit(solution)/shard_map/all_to_all | solution.py:76
  24.3 0.7 fusion.23
  25.0 0.0 copy-done
  25.0 2.0 %gather_fusion.1 = bf16[32,128,256]{2,1,0:T(8,128)(2,1)} fusion(bf16[32,128,256]{2,1,0:T(8,128)(2,1)S(1)} %copy-done, s32[1024]{0:T(1024)S(1)} %pad_clamp_fusion), kind=kCustom, calls=%fused_computation.1 | custom fusion | bytes 4194432 | tf_op jit(solution)/shard_map/jit(_take)/gather | solution.py:146
  27.0 0.0 copy-done.2
  27.0 3.3 %select_select_fusion = bf16[32,128,256]{2,1,0:T(8,128)(2,1)} fusion(bf16[32,128,256]{2,1,0:T(8,128)(2,1)} %gather_fusion.1, pred[32]{0:T(512)(128)(4,1)S(1)} %get-tuple-element.57, pred[32]{0:T(512)(128)(4,1)S(1)} %get-tuple-element.58), kind=kLoop, calls=%fused_computation.17 | loop fusion | flops 2097152 | bytes 4194368 | tf_op jit(solution)/shard_map/jit(_where)/select_n | solution.py:151
  30.3 0.0 copy-start.3
  30.3 0.0 copy-start.1
  30.3 1.8 %collective-permute-start = (bf16[32,128,256]{2,1,0:T(8,128)(2,1)}, bf16[32,128,256]{2,1,0:T(8,128)(2,1)}, u32[]{:S(2)}, u32[]{:S(2)}) collective-permute-start(bf16[32,128,256]{2,1,0:T(8,128)(2,1)} %select_select_fusion), channel_id=1, source_target_pairs={{248,0},{0,8},{8,16},{16,24},{24,32},{32,40},{40,48},{48,56},{56,6... | collective-permute-start | bytes 6291464 | tf_op jit(solution)/shard_map/ppermute | solution.py:16
  32.1 1.8 %reshape.267 = bf16[128,8,4,128]{3,2,1,0:T(4,128)(2,1)S(1)} reshape(bf16[128,4096]{1,0:T(8,128)(2,1)} %param.9) | data formatting | bytes 2097152 | tf_op jit(solution)/shard_map/reshape | solution.py:22
  33.9 2.0 %gather_fusion = bf16[32,128,256]{2,1,0:T(8,128)(2,1)} fusion(bf16[32,128,256]{2,1,0:T(8,128)(2,1)S(1)} %copy-done, s32[1024]{0:T(1024)S(1)} %pad_clamp_fusion.1), kind=kCustom, calls=%fused_computation | custom fusion | bytes 4194432 | tf_op jit(solution)/shard_map/jit(_take)/gather | solution.py:92
  35.9 0.0 copy-done.3
  35.9 0.6 fusion.22
  38.5 0.0 copy-done.1
  38.5 76.1 %all-gather = bf16[32,1,256]{2,1,0:T(2,128)(2,1)S(1)} all-gather(bf16[1,1,256]{2,1,0:T(2,128)(2,1)S(1)} %bitcast.147), channel_id=1, replica_groups=mesh['dp'=32,'seq'=8] {'dp'}, dimensions={0}, use_global_device_ids=true | all-gather | bytes 16896 | tf_op jit(solution)/shard_map/all_gather | solution.py:78
  114.6 0.1 broadcast_bitcast_fusion
  114.7 0.1 broadcast_compare_fusion
  114.8 2.9 %broadcast_select_fusion = bf16[1,4096,1,256]{3,1,2,0:T(8,128)(2,1)} fusion(bf16[1,4096,1,256]{3,1,2,0:T(8,128)(2,1)} %bitcast.140, pred[4096]{0:T(1024)(128)(4,1)S(1)} %broadcast_bitcast_fusion), kind=kLoop, calls=%fused_computation.18 | loop fusion | flops 1048576 | bytes 4198400 | tf_op jit(solution)/shard_map/jit(_take)/select_n | solution.py:92
  117.8 0.0 all-to-all-done
  117.8 1.7 %fusion.30 = (f32[4]{0:T(128)S(1)}, f32[4,4096]{1,0:T(4,128)S(1)}) fusion(bf16[1,4096,1,256]{3,1,2,0:T(8,128)(2,1)} %broadcast_select_fusion, bf16[512]{0:T(512)(128)(2,1)S(1)} %fusion.19, pred[4096]{0:T(1024)(128)(4,1)S(1)} %iota_compare_fusion.1), kind=kOutput, calls=%fused_computation.78 | convolution fusion | flops 4243452 | bytes 1119248 | tf_op jit(solution)/shard_map/rngd,rtnd->rngt/dot_general | solution.py:97
  119.5 0.1 fusion.31
  119.7 0.2 convert_reduce_fusion.2
  119.9 1.5 fusion.8
  121.4 0.6 copy.52
  122.0 0.0 collective-permute-done
  122.0 0.0 all-gather.3.cloned.1.call-done
  122.0 2.5 %fusion.29 = (bf16[512,2048]{0,1:T(8,128)(2,1)S(1)}, bf16[512,2048]{0,1:T(8,128)(2,1)S(1)}) fusion(bf16[1024,2048]{0,1:T(8,128)(2,1)} %all-gather.3.cloned.1.call-done), kind=kLoop, calls=%fused_computation.77 | loop fusion | bytes 8388608 | tf_op jit(solution)/shard_map/slice | solution.py:36
  124.5 2.1 %fusion = (f32[8,4,128]{2,1,0:T(4,128)S(1)}, f32[8,512,128,4]{2,1,3,0:T(8,128)S(1)}) fusion(pred[128,512]{0,1:T(8,128)(4,1)S(1)} %get-tuple-element.46, bf16[128,8,4,128]{3,2,1,0:T(4,128)(2,1)S(1)} %reshape.267, bf16[512,8,256]{0,2,1:T(8,128)(2,1)S(1)} %bitcast.143), kind=kOutput, calls=%fused_computation.8 | convolution fusion | flops 543158272 | bytes 10567680 | tf_op jit(solution)/shard_map/qngd,knd->ngqk/dot_general | solution.py:38
  126.6 2.1 %fusion.1 = (f32[8,4,128]{2,1,0:T(4,128)S(1)}, f32[8,512,128,4]{2,1,3,0:T(8,128)S(1)}) fusion(pred[128,512]{0,1:T(8,128)(4,1)S(1)} %get-tuple-element.45, bf16[128,8,4,128]{3,2,1,0:T(4,128)(2,1)S(1)} %reshape.267, bf16[512,8,256]{0,2,1:T(8,128)(2,1)S(1)} %bitcast.141), kind=kOutput, calls=%fused_computation.9 | convolution fusion | flops 543158272 | bytes 10567680 | tf_op jit(solution)/shard_map/qngd,knd->ngqk/dot_general | solution.py:38
  128.7 2.2 %fusion.11 = f32[8,4,128,128]{2,3,1,0:T(8,128)S(1)} fusion(bf16[512,8,256]{0,2,1:T(8,128)(2,1)S(1)} %bitcast.144, f32[8,512,128,4]{2,1,3,0:T(8,128)S(1)} %get-tuple-element.50, f32[8,4,128]{2,1,0:T(4,128)S(1)} %get-tuple-element.44, pred[128,512]{0,1:T(8,128)(4,1)S(1)} %get-tuple-element.46), kind=kOutput, calls=%fused_computation.31 | convolution fusion | flops 547356672 | bytes 11616256 | tf_op jit(solution)/shard_map/ngqk,knd->ngqd/dot_general | solution.py:53
  130.8 4.5 %convert_reduce_fusion = (f32[8,4,128]{2,1,0:T(4,128)S(1)}, f32[8,4,128]{2,1,0:T(4,128)S(1)}) fusion(f32[8,4,128]{2,1,0:T(4,128)S(1)} %get-tuple-element.43, f32[8,512,128,4]{2,1,3,0:T(8,128)S(1)} %get-tuple-element.48, pred[128,512]{0,1:T(8,128)(4,1)S(1)} %get-tuple-element.45, f32[8,4,128]{2,1,0:T(4,128)S(1)} %get-tuple-element.44, ...), kind=kLoop, calls=%fused_computation.4 | loop fusion | flops 29351936 | bytes 16973824 | tf_op jit(solution)/shard_map/reduce_sum | solution.py:52
  135.3 2.5 %fusion.4 = bf16[128,8,4,128]{0,3,2,1:T(8,128)(2,1)S(1)} fusion(f32[8,4,128,128]{2,3,1,0:T(8,128)S(1)} %fusion.11, bf16[512,8,256]{0,2,1:T(8,128)(2,1)S(1)} %bitcast.142, f32[128,8,4]{0,2,1:T(4,128)S(1)} %get-tuple-element.38, f32[128,8,4]{0,2,1:T(4,128)S(1)} %get-tuple-element.39, f32[128,8,4]{0,2,1:T(4,128)S(1)} %get-tuple-element.42, ...), kind=kOutput, calls=%fused_computation.14 | convolution fusion | flops 549978112 | bytes 12713984 | tf_op jit(solution)/shard_map/ngqk,knd->ngqd/dot_general | solution.py:53
  137.8 1.3 copy.33
  139.2 3.1 %copy.55 = bf16[32,128,256]{2,1,0:T(8,128)(2,1)} copy(bf16[32,128,256]{2,1,0:T(8,128)(2,1)} %collective-permute-done) | data formatting | bytes 4194304
  (16 shorter events, 0.2 us)
Async XLA Ops:
  7.2 17.8 %copy-start = (bf16[32,128,256]{2,1,0:T(8,128)(2,1)S(1)}, bf16[32,128,256]{2,1,0:T(8,128)(2,1)}, u32[]{:S(2)}) copy-start(bf16[32,128,256]{2,1,0:T(8,128)(2,1)} %param.14) | copy-start | bytes 6291460
  7.2 19.8 %copy-start.2 = (s32[1,32]{1,0:T(1,128)S(1)}, s32[1,32]{1,0:T(1,128)}, u32[]{:S(2)}) copy-start(s32[1,32]{1,0:T(1,128)} %param.15) | copy-start | bytes 388
  7.2 114.8 %all-gather.3.cloned.1.call-start = ((), (), s32[]{:S(2)}) async-start(), calls=%async_computation.1 | async-start | bytes 4718592 | tf_op jit(solution)/shard_map/all_gather | solution.py:27
  12.1 105.6 %all-to-all-start = ((bf16[32,2,256]{2,1,0:T(2,128)(2,1)}), bf16[32,2,256]{2,1,0:T(2,128)(2,1)S(1)}, u32[]{:S(2)}, u32[]{:S(2)}) async-start(bf16[32,2,256]{2,1,0:T(2,128)(2,1)} %reshape.358), calls=%async_computation | async-start | bytes 65536 | tf_op jit(solution)/shard_map/all_to_all | solution.py:76
  30.3 5.6 %copy-start.3 = (s32[32]{0:T(128)S(1)}, s32[32]{0:T(128)}, u32[]{:S(2)}) copy-start(s32[32]{0:T(128)} %param.13) | copy-start | bytes 388
  30.3 8.2 %copy-start.1 = (bf16[1,256]{1,0:T(2,128)(2,1)S(1)}, bf16[1,256]{1,0:T(2,128)(2,1)}, u32[]{:S(2)}) copy-start(bf16[1,256]{1,0:T(2,128)(2,1)} %param.12) | copy-start | bytes 1540
  30.3 91.7 %collective-permute-start = (bf16[32,128,256]{2,1,0:T(8,128)(2,1)}, bf16[32,128,256]{2,1,0:T(8,128)(2,1)}, u32[]{:S(2)}, u32[]{:S(2)}) collective-permute-start(bf16[32,128,256]{2,1,0:T(8,128)(2,1)} %select_select_fusion), channel_id=1, source_target_pairs={{248,0},{0,8},{8,16},{16,24},{24,32},{32,40},{40,48},{48,56},{56,6... | collective-permute-start | bytes 6291464 | tf_op jit(solution)/shard_map/ppermute | solution.py:16
Sparse Core Ops, SparseCore 0:
  10.4 40.3 all-gather.2
